TPU v7x, 256 devices: a whole 4x4x8 slice. The times are simulated.
256 devices in a mesh: segment: 16 (over y_lo, x, core), ctx: 16 (over y_hi, z).
Axes of the slice: x: 4, y: 4 (y_hi: 2, y_lo: 2; y = y_hi * 2 + y_lo), z: 8, core: 2. Of those that a mesh axis runs over, the one named last changes fastest.
Arguments:
- carried_down: bfloat16 [16, 2048, 1408], P('segment', 'ctx'), may hold values from -6 to 6
- carried_up: bfloat16 [16, 2048, 1408], P('segment', 'ctx'), may hold values from -6 to 6
- skip_bank: bfloat16 [16, 3, 2048, 1408], P('segment', None, 'ctx'), may hold values from -6 to 6
- queue: bfloat16 [8, 2048, 1408], P(None, 'ctx'), may hold values from -6 to 6
- next_entry: int32 [8], replicated, may hold values from 0 to 7, each once
- skip_slot: int32 [2, 16], P(None, 'segment'), may hold values from 0 to 2
- w_qkv: bfloat16 [16, 3, 1408, 1408], P('segment', None, 'ctx'), may hold values from -1.6523056 to 1.6523056
- w_out: bfloat16 [16, 1408, 1408], P('segment', 'ctx'), may hold values from -0.5 to 0.5
- w_skip: bfloat16 [16, 2816, 1408], P('segment', 'ctx'), may hold values from -0.109375 to 0.109375
- gains: float32 [16, 2, 1408], P('segment'), may hold values from 0.1 to 1.9
Outputs:
- desc_out: bfloat16 [2, 16, 2048, 1408], P(None, 'segment', 'ctx')
- asc_out: bfloat16 [2, 16, 2048, 1408], P(None, 'segment', 'ctx')
All inputs are finite; a program needn't handle non-finite values.
Results may differ from a plain program's by a relative error of at most 0.015.
Values may be sent and summed in bfloat16 or wider, within the bound.
A program may use at most 128 MiB of HBM per device.

v0:
```python
import jax
import jax.numpy as jnp
from jax import lax
from jax.sharding import PartitionSpec as P

HEAD = 88
D = 1408


def from_behind(value, axis, steps):
    count = lax.axis_size(axis)
    leading, last = (max(0, -steps), min(count, count - steps))
    return lax.ppermute(value, axis, [(source, source + steps) for source in range(leading, last)])


def layer_norm(values, gain):
    center = values - jnp.mean(values, axis=-1, keepdims=True)
    spread = jnp.mean(center * center, axis=-1, keepdims=True)
    return center * lax.rsqrt(spread + 1e-06) * gain


def attend(stacked):
    queries, keys, values = (stacked[0], stacked[1], stacked[2])
    local_heads, width, length = queries.shape
    block = 512
    blocks = length // block
    grouped = queries.reshape(local_heads, width, blocks, block).transpose(2, 0, 1, 3)

    def one_block(query_block):
        scores = jnp.einsum(
            "hen,hem->hnm", query_block, keys, preferred_element_type=jnp.float32
        ) * HEAD ** (-0.5)
        peak = jnp.max(scores, axis=2, keepdims=True)
        powers = jnp.exp(scores - peak)
        totals = jnp.sum(powers, axis=2)
        mixed = jnp.einsum(
            "hem,hnm->hen", values, powers.astype(jnp.bfloat16), preferred_element_type=jnp.float32
        )
        return (mixed / totals[:, None, :]).astype(jnp.bfloat16)

    results = lax.map(one_block, grouped)
    return results.transpose(1, 2, 0, 3).reshape(local_heads, width, length)


def send_down(descended):
    return from_behind(descended, "segment", 1)


def send_up(ascended):
    return from_behind(ascended, "segment", -1)


def on_device(
    carried_down, carried_up, skip_bank, queue, next_entry, skip_slot, w_qkv, w_out, w_skip, gains
):
    segment_count = lax.axis_size("segment")
    place = lax.axis_index("segment")
    tok_rows = carried_down.shape[1]
    local_heads = w_qkv.shape[2] // HEAD
    full_out, full_skip = (
        lax.all_gather(w_out[0], "ctx", axis=0, tiled=True),
        lax.all_gather(w_skip[0], "ctx", axis=0, tiled=True),
    )
    own_qkv = w_qkv[0].reshape(3, local_heads, HEAD, D)

    def descend(inputs):
        normed = layer_norm(inputs.astype(jnp.float32), gains[0, 0]).astype(jnp.bfloat16)
        made = jnp.einsum(
            "khed,td->khet",
            own_qkv,
            lax.all_gather(normed, "ctx", axis=0, tiled=True),
            preferred_element_type=jnp.float32,
        )
        projected = made.astype(jnp.bfloat16)
        head_out = attend(projected)
        returned = lax.all_to_all(head_out, "ctx", split_axis=2, concat_axis=0, tiled=True)
        merged = returned.reshape(D, tok_rows)
        added = jnp.einsum("ft,fd->td", merged, full_out, preferred_element_type=jnp.float32)
        return (inputs.astype(jnp.float32) + added).astype(jnp.bfloat16)

    def ascend(rising, slot):
        skip = lax.dynamic_index_in_dim(skip_bank[0], slot, 0, keepdims=False)
        joined = jnp.concatenate([rising, skip], axis=1)
        projected = jnp.dot(joined, full_skip, preferred_element_type=jnp.float32)
        return layer_norm(projected, gains[0, 1]).astype(jnp.bfloat16)

    first_down = descend(carried_down[0])
    first_up = ascend(carried_up[0], skip_slot[0, 0])
    arrive_down = send_down(first_down)
    arrive_up = send_up(first_up)
    entering = lax.dynamic_index_in_dim(queue, next_entry[0], 0, keepdims=False)
    down_next = jnp.where(place == 0, entering, arrive_down)
    up_next = jnp.where(place == segment_count - 1, first_down, arrive_up)
    second_down = descend(down_next)
    second_up = ascend(up_next, skip_slot[1, 0])
    desc_out = jnp.stack([first_down, second_down])[:, None]
    asc_out = jnp.stack([first_up, second_up])[:, None]
    return (desc_out, asc_out)


def solution(mesh):
    in_specs = (
        P("segment", "ctx", None),
        P("segment", "ctx", None),
        P("segment", None, "ctx", None),
        P(None, "ctx", None),
        P(),
        P(None, "segment"),
        P("segment", None, "ctx", None),
        P("segment", "ctx", None),
        P("segment", "ctx", None),
        P("segment", None, None),
    )
    out_specs = (P(None, "segment", "ctx", None), P(None, "segment", "ctx", None))
    return jax.shard_map(
        on_device, mesh=mesh, in_specs=in_specs, out_specs=out_specs, check_vma=False
    )
```

profile of v0, /device:TPU:2, one launch (start us, length us, event | category | flops | bytes accessed | tf_op | source)
XLA Modules:
  0.0 543.3 jit_solution(12254006201471091412)
XLA Ops:
  10.4 2.0 fusion.97
  20.7 105.8 %all-gather.7.cloned.1.call-done = bf16[2048,1408]{1,0:T(8,128)(2,1)} async-done(((bf16[128,1408]{1,0:T(8,128)(2,1)}), bf16[2048,1408]{1,0:T(8,128)(2,1)}) %all-gather.7.cloned.1.call-update) | async-done | bytes 5767184 | tf_op jit(solution)/shard_map/all_gather | solution.py:71
  126.6 4.5 fusion.73
  131.2 10.5 %while.20 = (s32[]{:T(128)}, bf16[4,1,88,512]{3,2,1,0:T(8,128)(2,1)S(1)}, bf16[4,1,88,512]{3,2,1,0:T(8,128)(2,1)S(1)}, bf16[1,88,2048]{2,1,0:T(8,128)(2,1)S(1)}, bf16[1,88,2048]{2,1,0:T(8,128)(2,1)S(1)}, /*index=5*/s32[]{:T(128)}) while((s32[]{:T(128)}, bf16[4,1,88,512]{3,2,1,0:T(8,128)(2,1)S(1)}, bf16[4,1,88,512]{3,2,1,0:T(8,128)(2,1)S(1)}, ...), condition=%wide.region_5.6_spmd, body=%wide.region_2.5_spmd.sunk | while | flops 377576448 | bytes 13494349 | solution.py:41
  142.8 11.5 %reduce.13 = bf16[2048,88]{1,0:T(8,128)(2,1)S(1)} reduce(bf16[2048,1,88]{2,1,0:T(2,128)(2,1)S(1)} %bitcast.194, bf16[]{:T(256)} %broadcast.140), dimensions={1}, to_apply=%bitcast.149.reduce_sub_computation | reduce | bytes 720898
  154.4 1.9 reshape.170
  156.3 4.3 all-to-all-start
  160.8 102.2 %all-gather.13.cloned.1.call-done = bf16[1,2816,1408]{2,1,0:T(8,128)(2,1)} async-done(((bf16[1,176,1408]{2,1,0:T(8,128)(2,1)}), bf16[1,2816,1408]{2,1,0:T(8,128)(2,1)}) %all-gather.13.cloned.1.call-update) | async-done | bytes 7929872 | tf_op jit(solution)/shard_map/all_gather | solution.py:62
  262.9 4.7 fusion.110
  268.7 1.9 collective-permute-start.1
  270.7 2.1 reshape.171
  273.6 87.3 %all-gather.11.cloned.1.call-done = bf16[1,1408,1408]{2,1,0:T(8,128)(2,1)} async-done(((bf16[1,88,1408]{2,1,0:T(8,128)(2,1)}), bf16[1,1408,1408]{2,1,0:T(8,128)(2,1)}) %all-gather.11.cloned.1.call-update) | async-done | bytes 3964944 | tf_op jit(solution)/shard_map/all_gather | solution.py:61
  361.0 3.1 broadcast_select_fusion
  364.1 1.9 collective-permute-start
  366.1 6.7 %collective-permute-done = bf16[128,1408]{1,0:T(8,128)(2,1)S(1)} collective-permute-done((bf16[128,1408]{1,0:T(8,128)(2,1)S(1)}, bf16[128,1408]{1,0:T(8,128)(2,1)S(1)}, u32[]{:S(2)}, u32[]{:S(2)}) %collective-permute-start) | collective-permute-done | bytes 360480 | tf_op jit(solution)/shard_map/ppermute | solution.py:13
  376.2 4.7 fusion.111
  382.0 101.1 %all-gather.9.cloned.1.call-done = bf16[2048,1408]{1,0:T(8,128)(2,1)} async-done(((bf16[128,1408]{1,0:T(8,128)(2,1)}), bf16[2048,1408]{1,0:T(8,128)(2,1)}) %all-gather.9.cloned.1.call-update) | async-done | bytes 5767184 | tf_op jit(solution)/shard_map/all_gather | solution.py:71
  483.0 4.5 fusion.70
  487.7 10.7 %while.21 = (s32[]{:T(128)}, bf16[4,1,88,512]{3,2,1,0:T(8,128)(2,1)S(1)}, bf16[4,1,88,512]{3,2,1,0:T(8,128)(2,1)S(1)}, bf16[1,88,2048]{2,1,0:T(8,128)(2,1)S(1)}, bf16[1,88,2048]{2,1,0:T(8,128)(2,1)S(1)}, /*index=5*/s32[]{:T(128)}) while((s32[]{:T(128)}, bf16[4,1,88,512]{3,2,1,0:T(8,128)(2,1)S(1)}, bf16[4,1,88,512]{3,2,1,0:T(8,128)(2,1)S(1)}, ...), condition=%wide.region_11.12_spmd, body=%wide.region_8.11_spmd.sunk | while | flops 377576448 | bytes 13494349 | solution.py:41
  499.0 11.5 %reduce.14 = bf16[2048,88]{1,0:T(8,128)(2,1)S(1)} reduce(bf16[2048,1,88]{2,1,0:T(2,128)(2,1)S(1)} %bitcast.195, bf16[]{:T(256)} %broadcast.140), dimensions={1}, to_apply=%bitcast.151.reduce_sub_computation | reduce | bytes 720898
  512.4 4.3 all-to-all-start.1
  516.8 11.4 %all-to-all-done.1 = bf16[16,2,5632]{2,1,0:T(2,128)(2,1)} async-done(((bf16[16,2,5632]{2,1,0:T(2,128)(2,1)}), bf16[16,2,5632]{2,1,0:T(2,128)(2,1)}, u32[]{:S(2)}, u32[]{:S(2)}) %all-to-all-start.1) | async-done | bytes 360480 | tf_op jit(solution)/shard_map/all_to_all | solution.py:76
  528.3 3.4 reshape.173
  532.5 2.9 fusion.82
  (96 shorter events, 41.3 us)
Async XLA Ops:
  7.2 119.4 %copy-start = (bf16[1,3,88,1408]{3,2,1,0:T(8,128)(2,1)S(1)}, bf16[1,3,88,1408]{3,2,1,0:T(8,128)(2,1)}, u32[]{:S(2)}) copy-start(bf16[1,3,88,1408]{3,2,1,0:T(8,128)(2,1)} %param.20) | copy-start | bytes 2230276
  7.2 119.4 %all-gather.7.cloned.1.call-start = ((), (), s32[]{:S(2)}) async-start(), calls=%async_computation.2 | async-start | bytes 6127616 | tf_op jit(solution)/shard_map/all_gather | solution.py:71
  12.4 250.5 %all-gather.13.cloned.1.call-start = ((), (), s32[]{:S(2)}) async-start(), calls=%async_computation.5 | async-start | bytes 8425472 | tf_op jit(solution)/shard_map/all_gather | solution.py:62
  13.2 347.8 %all-gather.11.cloned.1.call-start = ((), (), s32[]{:S(2)}) async-start(), calls=%async_computation.4 | async-start | bytes 4212736 | tf_op jit(solution)/shard_map/all_gather | solution.py:61
  141.7 121.2 %copy-start.9 = (bf16[1,128,1408]{2,1,0:T(8,128)(2,1)S(1)}, bf16[1,128,1408]{2,1,0:T(8,128)(2,1)}, u32[]{:S(2)}) copy-start(bf16[1,128,1408]{2,1,0:T(8,128)(2,1)} %param.15) | copy-start | bytes 1081348
  156.3 114.4 %all-to-all-start = ((bf16[16,2,5632]{2,1,0:T(2,128)(2,1)}), bf16[16,2,5632]{2,1,0:T(2,128)(2,1)S(1)}, u32[]{:S(2)}, u32[]{:S(2)}) async-start(bf16[16,2,5632]{2,1,0:T(2,128)(2,1)} %reshape.170), calls=%async_computation | async-start | bytes 720896 | tf_op jit(solution)/shard_map/all_to_all | solution.py:76
  160.5 322.5 %all-gather.9.cloned.1.call-start = ((), (), s32[]{:S(2)}) async-start(), calls=%async_computation.3 | async-start | bytes 6127616 | tf_op jit(solution)/shard_map/all_gather | solution.py:71
  267.6 93.4 %copy-start.1 = (bf16[1,128,1408]{2,1,0:T(8,128)(2,1)S(1)}, bf16[1,128,1408]{2,1,0:T(8,128)(2,1)}, u32[]{:S(2)}) copy-start(bf16[1,128,1408]{2,1,0:T(8,128)(2,1)} %param.14) | copy-start | bytes 1081348
  268.7 92.2 %collective-permute-start.1 = (bf16[128,1408]{1,0:T(8,128)(2,1)}, bf16[128,1408]{1,0:T(8,128)(2,1)}, u32[]{:S(2)}, u32[]{:S(2)}) collective-permute-start(bf16[128,1408]{1,0:T(8,128)(2,1)} %multiply_convert_fusion.1), channel_id=1, source_target_pairs={{16,0},{32,16},{48,32},{64,48},{80,64},{96,80},{112,96},{128,112},... | collective-permute-start | bytes 1081352 | tf_op jit(solution)/shard_map/ppermute | solution.py:13
  273.4 92.6 %copy-start.8 = (s32[8]{0:T(128)S(1)}, s32[8]{0:T(128)}, u32[]{:S(2)}) copy-start(s32[8]{0:T(128)} %param.18) | copy-start | bytes 100
  361.0 15.2 %copy-start.7 = (bf16[128,1408]{1,0:T(8,128)(2,1)S(1)}, bf16[128,1408]{1,0:T(8,128)(2,1)}, u32[]{:S(2)}) copy-start(bf16[128,1408]{1,0:T(8,128)(2,1)} %get-tuple-element.95) | copy-start | bytes 1081348
  364.1 16.8 %copy-start.5 = (bf16[128,1408]{1,0:T(8,128)(2,1)}, bf16[128,1408]{1,0:T(8,128)(2,1)S(1)}, u32[]{:S(2)}) copy-start(bf16[128,1408]{1,0:T(8,128)(2,1)S(1)} %get-tuple-element.107) | copy-start | bytes 1081348
  364.1 8.7 %collective-permute-start = (bf16[128,1408]{1,0:T(8,128)(2,1)S(1)}, bf16[128,1408]{1,0:T(8,128)(2,1)S(1)}, u32[]{:S(2)}, u32[]{:S(2)}) collective-permute-start(bf16[128,1408]{1,0:T(8,128)(2,1)S(1)} %get-tuple-element.107), channel_id=1, source_target_pairs={{0,16},{16,32},{32,48},{48,64},{64,80},{80,96},{96,112},{112,128},... | collective-permute-start | bytes 1081352 | tf_op jit(solution)/shard_map/ppermute | solution.py:13
  380.9 0.9 copy-start.2
  498.4 18.3 %copy-start.3 = (f32[128,1408]{1,0:T(8,128)S(1)}, f32[128,1408]{1,0:T(8,128)}, u32[]{:S(2)}) copy-start(f32[128,1408]{1,0:T(8,128)} %copy-done.2) | copy-start | bytes 2162692
  512.4 15.9 %all-to-all-start.1 = ((bf16[16,2,5632]{2,1,0:T(2,128)(2,1)}), bf16[16,2,5632]{2,1,0:T(2,128)(2,1)}, u32[]{:S(2)}, u32[]{:S(2)}) async-start(bf16[16,2,5632]{2,1,0:T(2,128)(2,1)} %reshape.172), calls=%async_computation.1 | async-start | bytes 720896 | tf_op jit(solution)/shard_map/all_to_all | solution.py:76
  531.6 3.8 copy-start.4
  532.3 3.2 copy-start.6
Sparse Core Ops, SparseCore 0:
  12.5 113.9 all-gather.6
  129.2 133.6 all-gather.12
  265.6 95.3 all-gather.10
  375.4 107.5 all-gather.8
where the time goes:
time: 544 us; the launch traced here: 543 us
  waiting for transfers between devices  416 us (76%)
  other arithmetic  40.2 us (7%)
  matrix products  38.6 us (7%)
  between operations  17.9 us (3%)
  local copies, waits for them, and re-layouts  17.5 us (3%)
  starting transfers between devices  12.7 us (2%)
    all_gather x2, waiting for transfers between devices, descend(): lax.all_gather(normed, 'ctx', axis=0, tiled=True)  207 us
    all_gather x1, waiting for transfers between devices, on_device(): lax.all_gather(w_skip[0], 'ctx', axis=0, tiled=True)  102 us
    all_gather x1, waiting for transfers between devices, on_device(): lax.all_gather(w_out[0], 'ctx', axis=0, tiled=True)  87.3 us
    unnamed x3, other arithmetic  24.3 us
    all_to_all x2, waiting for transfers between devices, descend(): lax.all_to_all(head_out, 'ctx', split_axis=2, concat_axis=0, tiled=True)  11.4 us
  transfers between devices with their start and end apart: 8, of which 6 were waited for; matrix products, arithmetic and copies ran while one was open for 9% of the time, Pallas kernels for 0%

commit v1 on v0

v1 whole, which is shorter than its diff:
```python
import jax
import jax.numpy as jnp
from jax import lax
from jax.experimental import pallas as pl
from jax.experimental.pallas import tpu as pltpu
from jax.sharding import PartitionSpec as P

HEAD = 88
HP = 96
D = 1408
TOK = 128
RING = 8
SEGS = 16
ROWS = 176
SCALE = HEAD**-0.5
LOG2E = 1.4426950408889634
MESH = pl.DeviceIdType.MESH
BF = jnp.bfloat16
F32 = jnp.float32
GROUPS = ((0, 1), (1, 3), (3, 5), (5, 7), (7, 8))


def slot_of(delta):
    if delta == 0:
        return 0
    if abs(delta) == 4:
        return 7
    return 2 * delta - 1 if delta > 0 else -2 * delta


def nt(a, b):
    return lax.dot_general(a, b, (((1,), (1,)), ((), ())), preferred_element_type=F32)


def tn(a, b):
    return lax.dot_general(a, b, (((0,), (0,)), ((), ())), preferred_element_type=F32)


def layer_norm(x, gain):
    center = x - jnp.mean(x, axis=-1, keepdims=True)
    spread = jnp.mean(center * center, axis=-1, keepdims=True)
    return center * lax.rsqrt(spread + 1e-06) * gain


class Ring:
    def __init__(self, peers, send, recv, src, dst):
        self.peers, self.send, self.recv, self.src, self.dst = peers, send, recv, src, dst

    def copy(self, way, j):
        hops, half = j // 2, (way if j == 6 else j % 2)
        return pltpu.make_async_remote_copy(
            self.src(way, hops, half),
            self.dst(way, hops, half),
            self.send.at[way, j],
            self.recv.at[way, j],
            device_id={"ctx": self.peers[way]},
            device_id_type=MESH,
        )

    def start(self, way, j):
        self.copy(way, j).start()

    def arrive(self, way, j):
        hops, half = j // 2, (way if j == 6 else j % 2)
        here = self.src(way, hops + 1, half)
        pltpu.make_async_remote_copy(
            here,
            here,
            self.send.at[way, j],
            self.recv.at[way, j],
            device_id={"ctx": self.peers[way]},
            device_id_type=MESH,
        ).wait_recv()

    def begin(self, half):
        self.start(0, half)
        self.start(1, half)

    def step(self, j):
        for way in (0, 1):
            self.arrive(way, j)
            if j < 4:
                self.start(way, j + 2)
            elif j == 4 + way:
                self.start(way, 6)

    def drain(self):
        for way in (0, 1):
            for j in range(7):
                self.copy(way, j).wait_send()


def slot_ring(peers, send, recv, view):
    def src(way, hops, half):
        return view(slot_of(-hops if way == 0 else hops), half)

    def dst(way, hops, half):
        return view(slot_of(-hops - 1 if way == 0 else hops + 1), half)

    return Ring(peers, send, recv, src, dst)


def row_ring(peers, send, recv, z, buf):
    def src(way, hops, half):
        origin = lax.rem(z + (8 - hops if way == 0 else hops), 8)
        start = pl.multiple_of(origin * ROWS + half * 96, 16)
        return buf.at[pl.ds(start, 80 if half else 96), :]

    return Ring(peers, send, recv, src, src)


def kernel(
    x_in, up_in, bank_in, queue_in, entry, slots, qkv_in, out_in, skip_in, gains,
    desc_ref, asc_ref,
    xs, down, bank, queue, stage_qkv, act, wqv, wk, qt, kk, vt, qs, ks, vs, scores, ot, mt,
    wo, wsk, part_send, part_recv, x1, operand, give, asc_send, asc_recv, asc_out,
    load, store, act_send, act_recv, wo_send, wo_recv, wsk_send, wsk_recv,
    pair_send, pair_recv, w_send, w_recv, head_send, head_recv,
    part_ss, part_rs, down_ss, down_rs, give_ss, give_rs, rise_ss, rise_rs, mix_ss, mix_rs,
):
    s = lax.axis_index("segment")
    c = lax.axis_index("ctx")
    y, z = c // 8, c % 8
    partner = (1 - y) * 8 + z
    above, below = (s + 1) % SEGS, (s + SEGS - 1) % SEGS

    def ring_peer(delta):
        return y * 8 + (z + delta + 8) % 8

    peers = (ring_peer(1), ring_peer(-1))

    loads = [
        pltpu.make_async_copy(x_in, xs.at[0], load.at[0]),
        pltpu.make_async_copy(qkv_in, stage_qkv, load.at[1]),
        pltpu.make_async_copy(out_in, wo.at[0, pl.ds(0, HEAD), :], load.at[2]),
        pltpu.make_async_copy(skip_in, wsk.at[pl.ds(pl.multiple_of(z * ROWS, 16), ROWS), :], load.at[3]),
        pltpu.make_async_copy(up_in, xs.at[2], load.at[4]),
        pltpu.make_async_copy(bank_in, bank, load.at[5]),
        pltpu.make_async_copy(queue_in, queue, load.at[6]),
    ]
    for copy in loads:
        copy.start()

    barrier = pltpu.get_barrier_semaphore()
    diagonal = {"segment": (s + SEGS + 1 - 2 * y) % SEGS, "ctx": partner}
    greet = [{"ctx": ring_peer(d)} for d in (1, -1, 2, -2, 3, -3, 4)]
    greet += [{"ctx": partner}, {"segment": above}, {"segment": below}, diagonal]
    for peer in greet:
        pl.semaphore_signal(barrier, inc=1, device_id=peer, device_id_type=MESH)

    wo[0, HEAD:HP, :] = jnp.zeros((HP - HEAD, D), BF)
    for block in range(2):
        wqv[block * HP + HEAD : (block + 1) * HP, :] = jnp.zeros((HP - HEAD, D), BF)
    wk[HEAD:128, :] = jnp.zeros((128 - HEAD, D), BF)
    wk[128 + HP : 256, :] = jnp.zeros((128 - HP, D), BF)
    qt[:, :, HP:128, :] = jnp.zeros((2, RING, 128 - HP, 256), BF)

    gain_down, gain_up = gains[0:1, :], gains[1:2, :]
    loads[0].wait()
    act[0, 0] = layer_norm(xs[0].astype(F32), gain_down).astype(BF)
    pl.semaphore_wait(barrier, len(greet))

    def act_ring(t):
        return slot_ring(
            peers, act_send.at[t], act_recv.at[t],
            lambda p, half: act.at[t, p, pl.ds(half * 64, 64), :],
        )

    rings = [act_ring(0), act_ring(1)]
    out_ring = slot_ring(peers, wo_send, wo_recv, lambda p, half: wo.at[p, pl.ds(half * 48, 48), :])
    skip_ring = row_ring(peers, wsk_send, wsk_recv, z, wsk)

    rings[0].begin(0)
    rings[0].begin(1)

    def to_partner(src, dst, send, recv):
        return pltpu.make_async_remote_copy(
            src, dst, send, recv, device_id={"ctx": partner}, device_id_type=MESH
        )

    loads[1].wait()
    wqv[0:HEAD, :] = stage_qkv[0]
    wqv[HP : HP + HEAD, :] = stage_qkv[2]
    wk[0:HEAD, :] = stage_qkv[1]
    w_copies = [
        to_partner(wqv.at[pl.ds(0, 2 * HP), :], wqv.at[pl.ds(2 * HP, 2 * HP), :], w_send.at[0], w_recv.at[0]),
        to_partner(wk.at[pl.ds(0, HP), :], wk.at[pl.ds(128, HP), :], w_send.at[1], w_recv.at[1]),
    ]
    for copy in w_copies:
        copy.start()

    loads[4].wait()
    loads[5].wait()
    skip_first = bank[slots[0, 0]]
    skip_second = bank[slots[1, 0]]
    rising = xs[2]
    operand[0, 0:TOK, :] = jnp.where(y == 0, rising, skip_first)
    give[0] = jnp.where(y == 0, skip_first, rising)
    give[1] = skip_second
    give_copies = [
        to_partner(give.at[t], operand.at[t, pl.ds(TOK, TOK), :], give_ss.at[t], give_rs.at[t])
        for t in range(2)
    ]

    @pl.when(y == 1)
    def _():
        operand[1, 0:TOK, :] = skip_second

    def pair_copies(t, g):
        lo, hi = GROUPS[g]
        n = (hi - lo) * TOK
        return [
            to_partner(
                qs.at[t, pl.ds(lo, hi - lo)],
                qt.at[t, pl.ds(lo, hi - lo), pl.ds(0, HP), pl.ds(128, 128)],
                pair_send.at[t, g, 0], pair_recv.at[t, g, 0],
            ),
            to_partner(
                ks.at[t, pl.ds(lo * TOK, n), :],
                kk.at[t, pl.ds(1024 + lo * TOK, n), :],
                pair_send.at[t, g, 1], pair_recv.at[t, g, 1],
            ),
            to_partner(
                vs.at[t, :, pl.ds(lo * TOK, n)],
                vt.at[t, :, pl.ds(1024 + lo * TOK, n)],
                pair_send.at[t, g, 2], pair_recv.at[t, g, 2],
            ),
        ]

    def project(t, g):
        lo, hi = GROUPS[g]
        n = (hi - lo) * TOK
        tokens = act[t, lo:hi].reshape(n, D)
        made = nt(wqv[...], tokens)
        keys = nt(tokens, wk[...]).astype(BF)
        one = lax.broadcasted_iota(jnp.int32, (HP, n), 0) == HEAD
        own_v = jnp.where(one, 1.0, made[HP : 2 * HP]).astype(BF)
        pair_v = jnp.where(one, 1.0, made[3 * HP : 4 * HP]).astype(BF)
        made = made.astype(BF)
        for p in range(lo, hi):
            cols = slice((p - lo) * TOK, (p - lo + 1) * TOK)
            qt[t, p, 0:HP, 0:128] = made[0:HP, cols]
            qs[t, p] = made[2 * HP : 3 * HP, cols]
        vt[t, :, lo * TOK : hi * TOK] = own_v
        vs[t, :, lo * TOK : hi * TOK] = pair_v
        kk[t, lo * TOK : hi * TOK, :] = keys[:, 0:128]
        ks[t, lo * TOK : hi * TOK, :] = keys[:, 128:256]
        for copy in pair_copies(t, g):
            copy.start()

    def head_copy(t, p, mirror, delta):
        return pltpu.make_async_remote_copy(
            ot.at[t, p], mt.at[t, mirror], head_send.at[t, p], head_recv.at[t, mirror],
            device_id={"ctx": y * 8 + (z + delta + 8) % 8}, device_id_type=MESH,
        )

    def attend_block(t, p):
        queries = qt[t, p]
        peak = None
        for kb in range(8):
            made = jnp.dot(kk[t, kb * 256 : (kb + 1) * 256, :], queries, preferred_element_type=F32)
            scores[kb] = made
            top = jnp.max(made.reshape(32, 8, 256), axis=0)
            peak = top if peak is None else jnp.maximum(peak, top)
        peak = jnp.max(peak, axis=0, keepdims=True)
        total = jnp.zeros((HP, 256), F32)
        for kb in range(8):
            powers = jnp.exp2((scores[kb] - peak) * (SCALE * LOG2E)).astype(BF)
            total += jnp.dot(vt[t, :, kb * 256 : (kb + 1) * 256], powers, preferred_element_type=F32)
        return (total * (1.0 / total[HEAD : HEAD + 1, :])).astype(BF)

    def attend(t, between):
        def body(i, carry):
            p = 7 - i
            ot[t, p] = attend_block(t, p)
            odd = p % 2
            delta = ((p + 1) // 2) * (2 * odd - 1)
            mirror = p + (2 * odd - 1) * (1 - p // 7)

            @pl.when(p > 0)
            def _():
                head_copy(t, p, mirror, delta).start()

            for at, work in between.items():

                @pl.when(i == at)
                def _():
                    work()

            return carry

        lax.fori_loop(0, 8, body, 0)
        mt[t, 0] = ot[t, 0]

    def out_project(t):
        for p in range(1, 8):
            head_copy(t, p, p, 0).wait_recv()
        weights = wo[...].reshape(RING * HP, D)
        heads = mt[t].reshape(RING * HP, 256)
        part_send[t] = tn(heads[:, 128:256], weights).astype(BF)
        copies = [
            to_partner(
                part_send.at[t, pl.ds(h * 64, 64), :], part_recv.at[t, pl.ds(h * 64, 64), :],
                part_ss.at[t, h], part_rs.at[t, h],
            )
            for h in range(2)
        ]
        for copy in copies:
            copy.start()
        own = tn(heads[:, 0:128], weights) + xs[t].astype(F32)
        return own, copies

    def down_copy(h):
        return pltpu.make_async_remote_copy(
            x1.at[0, pl.ds(h * 64, 64), :], down.at[pl.ds(h * 64, 64), :],
            down_ss.at[h], down_rs.at[h], device_id={"segment": above}, device_id_type=MESH,
        )

    def rise_copy():
        return pltpu.make_async_remote_copy(
            asc_out.at[0], operand.at[1, pl.ds(pl.multiple_of(y * TOK, 16), TOK), :],
            rise_ss.at[0], rise_rs.at[y], device_id={"segment": below, "ctx": z}, device_id_type=MESH,
        )

    def turn_copy():
        return pltpu.make_async_remote_copy(
            x1.at[0], operand.at[1, pl.ds(TOK, TOK), :],
            rise_ss.at[1], rise_rs.at[1], device_id={"ctx": partner}, device_id_type=MESH,
        )

    def mix_copy(t):
        return to_partner(asc_send.at[t], asc_recv.at[t], mix_ss.at[t], mix_rs.at[t])

    def ascend_first(t):
        asc_send[t] = jnp.dot(operand[t, TOK : 2 * TOK, :], wsk[...], preferred_element_type=F32).astype(BF)
        mix_copy(t).start()
        return jnp.dot(operand[t, 0:TOK, :], wsk[...], preferred_element_type=F32)

    def ascend_last(t, own):
        mix_copy(t).wait_recv()
        asc_out[t] = layer_norm(own + asc_recv[t].astype(F32), gain_up).astype(BF)
        pltpu.make_async_copy(asc_out.at[t], asc_ref.at[t], store.at[1, t]).start()

    for j in range(7):
        rings[0].step(j)
        if j == 1:
            for copy in w_copies:
                copy.wait_recv()
            project(0, 0)
            project(0, 1)
            give_copies[0].start()
            pl.when(y == 0)(lambda: give_copies[1].start())
        if j == 3:
            project(0, 2)
        if j == 5:
            loads[2].wait()
            out_ring.begin(0)
            out_ring.begin(1)
            project(0, 3)
        if j == 6:
            project(0, 4)
    for g in range(5):
        for copy in pair_copies(0, g):
            copy.wait_recv()
    attend(0, {1: lambda: out_ring.step(0), 3: lambda: out_ring.step(1), 5: lambda: out_ring.step(2), 7: lambda: out_ring.step(3)})
    for j in range(4, 7):
        out_ring.step(j)
    loads[3].wait()
    skip_ring.begin(0)
    skip_ring.begin(1)
    own, copies = out_project(0)
    skip_ring.step(0)
    skip_ring.step(1)
    for h in range(2):
        rows = slice(h * 64, (h + 1) * 64)
        copies[h].wait_recv()
        x1[0, rows, :] = (own[rows] + part_recv[0, rows, :].astype(F32)).astype(BF)
        down_copy(h).start()
    pltpu.make_async_copy(x1.at[0], desc_ref.at[0], store.at[0, 0]).start()

    last = s == SEGS - 1

    @pl.when(jnp.logical_and(last, y == 0))
    def _():
        operand[1, 0:TOK, :] = x1[0]

    @pl.when(jnp.logical_and(last, y == 1))
    def _():
        turn_copy().start()

    loads[6].wait()
    entering = queue[entry[0]]
    for h in range(2):
        rows = slice(h * 64, (h + 1) * 64)
        down_copy(h).wait_recv()
        xs[1, rows, :] = jnp.where(s == 0, entering[rows], down[rows, :])
        act[1, 0, rows, :] = layer_norm(xs[1, rows, :].astype(F32), gain_down).astype(BF)
        rings[1].begin(h)
    project(1, 0)
    skip_ring.step(2)
    skip_ring.step(3)
    for j in range(7):
        rings[1].step(j)
        if j == 1:
            project(1, 1)
            skip_ring.step(4)
        if j == 3:
            project(1, 2)
            skip_ring.step(5)
        if j == 5:
            project(1, 3)
            skip_ring.step(6)
        if j == 6:
            project(1, 4)

    give_copies[0].wait_recv()
    own_up = ascend_first(0)
    for g in range(5):
        for copy in pair_copies(1, g):
            copy.wait_recv()
    ascend_last(0, own_up)

    @pl.when(s > 0)
    def _():
        rise_copy().start()

    attend(1, {})

    own, copies = out_project(1)

    @pl.when(y == 1)
    def _():
        give_copies[1].wait_recv()

    @pl.when(jnp.logical_and(y == 0, s < SEGS - 1))
    def _():
        pltpu.make_async_remote_copy(
            asc_out.at[0], operand.at[1, pl.ds(0, TOK), :], rise_ss.at[0], rise_rs.at[0],
            device_id={"segment": below, "ctx": z}, device_id_type=MESH,
        ).wait_recv()

    @pl.when(y == 0)
    def _():
        turn_copy().wait_recv()

    own_up = ascend_first(1)
    for h in range(2):
        rows = slice(h * 64, (h + 1) * 64)
        copies[h].wait_recv()
        x1[1, rows, :] = (own[rows] + part_recv[1, rows, :].astype(F32)).astype(BF)
    pltpu.make_async_copy(x1.at[1], desc_ref.at[1], store.at[0, 1]).start()
    ascend_last(1, own_up)

    for ring in (*rings, out_ring, skip_ring):
        ring.drain()
    for copy in w_copies:
        copy.wait_send()
    give_copies[0].wait_send()
    pl.when(y == 0)(lambda: give_copies[1].wait_send())
    for t in range(2):
        for g in range(5):
            for copy in pair_copies(t, g):
                copy.wait_send()
        for p in range(1, 8):
            head_copy(t, p, p, 0).wait_send()
        for h in range(2):
            to_partner(
                part_send.at[t, pl.ds(h * 64, 64), :], part_recv.at[t, pl.ds(h * 64, 64), :],
                part_ss.at[t, h], part_rs.at[t, h],
            ).wait_send()
        mix_copy(t).wait_send()
    for h in range(2):
        down_copy(h).wait_send()
    pl.when(s > 0)(lambda: rise_copy().wait_send())
    pl.when(jnp.logical_and(last, y == 1))(lambda: turn_copy().wait_send())
    for t in range(2):
        pltpu.make_async_copy(x1.at[t], desc_ref.at[t], store.at[0, t]).wait()
        pltpu.make_async_copy(asc_out.at[t], asc_ref.at[t], store.at[1, t]).wait()


def on_device(
    carried_down, carried_up, skip_bank, queue, next_entry, skip_slot, w_qkv, w_out, w_skip, gains
):
    hbm = pl.BlockSpec(memory_space=pl.ANY)
    smem = pl.BlockSpec(memory_space=pltpu.SMEM)
    vmem = pl.BlockSpec(memory_space=pltpu.VMEM)
    dma = pltpu.SemaphoreType.DMA
    V = pltpu.VMEM
    scratch = [
        V((3, TOK, D), BF),
        V((TOK, D), BF),
        V((3, TOK, D), BF),
        V((8, TOK, D), BF),
        V((3, HEAD, D), BF),
        V((2, RING, TOK, D), BF),
        V((4 * HP, D), BF),
        V((256, D), BF),
        V((2, RING, 128, 256), BF),
        V((2, 2048, 128), BF),
        V((2, HP, 2048), BF),
        V((2, RING, HP, 128), BF),
        V((2, 1024, 128), BF),
        V((2, HP, 1024), BF),
        V((8, 256, 256), F32),
        V((2, RING, HP, 256), BF),
        V((2, RING, HP, 256), BF),
        V((RING, HP, D), BF),
        V((D, D), BF),
        V((2, TOK, D), BF),
        V((2, TOK, D), BF),
        V((2, TOK, D), BF),
        V((2, 2 * TOK, D), BF),
        V((2, TOK, D), BF),
        V((2, TOK, D), BF),
        V((2, TOK, D), BF),
        V((2, TOK, D), BF),
        dma((7,)), dma((2, 2)),
        dma((2, 2, 7)), dma((2, 2, 7)), dma((2, 7)), dma((2, 7)), dma((2, 7)), dma((2, 7)),
        dma((2, 5, 3)), dma((2, 5, 3)), dma((2,)), dma((2,)), dma((2, 8)), dma((2, 8)),
        dma((2, 2)), dma((2, 2)), dma((2,)), dma((2,)), dma((2,)), dma((2,)),
        dma((2,)), dma((2,)), dma((2,)), dma((2,)),
    ]
    desc, asc = pl.pallas_call(
        kernel,
        out_shape=(
            jax.ShapeDtypeStruct((2, TOK, D), BF),
            jax.ShapeDtypeStruct((2, TOK, D), BF),
        ),
        in_specs=[hbm, hbm, hbm, hbm, smem, smem, hbm, hbm, hbm, vmem],
        out_specs=(hbm, hbm),
        scratch_shapes=scratch,
        compiler_params=pltpu.CompilerParams(
            collective_id=0, has_side_effects=True, vmem_limit_bytes=60 * 1024 * 1024
        ),
    )(
        carried_down[0], carried_up[0], skip_bank[0], queue, next_entry, skip_slot,
        w_qkv[0], w_out[0], w_skip[0], gains[0],
    )
    return desc[:, None], asc[:, None]


def solution(mesh):
    in_specs = (
        P("segment", "ctx", None),
        P("segment", "ctx", None),
        P("segment", None, "ctx", None),
        P(None, "ctx", None),
        P(),
        P(None, "segment"),
        P("segment", None, "ctx", None),
        P("segment", "ctx", None),
        P("segment", "ctx", None),
        P("segment", None, None),
    )
    out_specs = (P(None, "segment", "ctx", None), P(None, "segment", "ctx", None))
    return jax.shard_map(
        on_device, mesh=mesh, in_specs=in_specs, out_specs=out_specs, check_vma=False
    )
```

time: 544 us -> 206 us (0.38)
  waiting for transfers between devices: 416 us -> 0 us
  Pallas kernels: 0 us -> 196 us
  other arithmetic: 40.2 us -> 0 us
  matrix products: 38.6 us -> 0 us
  between operations: 17.9 us -> 0.64 us
  starting transfers between devices: 12.7 us -> 0 us
  local copies, waits for them, and re-layouts: 17.5 us -> 5.34 us
    all_gather x4 -> x0, waiting for transfers between devices: 396 us -> none  [the longest x2 207 us: descend(): lax.all_gather(normed, 'ctx', axis=0, tiled=True)]
    pallas_call x0 -> x1, Pallas kernels: none -> 196 us  [on_device(): pl.pallas_call(kernel, out_shape=(jax.ShapeDtypeStruct((2, TOK, D), BF),...]
    dot_general x22 -> x0, matrix products: 38.6 us -> none  [the longest x2 9.3 us: ascend(): projected = jnp.dot(joined, full_skip, preferred_element_type=jnp.float32)]
    unnamed x3 -> x0, other arithmetic: 24.3 us -> none
    all_to_all x2 -> x0, waiting for transfers between devices: 11.4 us -> none  [descend(): lax.all_to_all(head_out, 'ctx', split_axis=2, concat_axis=0, tiled=True)]
    reduce_sum x14 -> x0, other arithmetic: 10.8 us -> none  [the longest x8 6.59 us: one_block(): totals = jnp.sum(powers, axis=2)]
    all_to_all x2 -> x0, starting transfers between devices: 8.55 us -> none  [descend(): lax.all_to_all(head_out, 'ctx', split_axis=2, concat_axis=0, tiled=True)]
    ppermute x2 -> x0, waiting for transfers between devices: 6.7 us -> none  [from_behind(): lax.ppermute(value, axis, [(source, source + steps) for source in range(l...]
  transfers between devices with their start and end apart: 8 -> 0, of which waited for: 6 -> 0; matrix products, arithmetic and copies ran while one was open for 9% -> 0% of each run, Pallas kernels for 0% -> 0%
where the time goes in v1:
time: 206 us; the launch traced here: 202 us
  Pallas kernels  196 us (95%)
  local copies, waits for them, and re-layouts  5.34 us (3%)
    pallas_call x1, Pallas kernels, on_device(): pl.pallas_call(kernel, out_shape=(jax.ShapeDtypeStruct((2, TOK, D), BF),...  196 us
    unnamed x3, local copies, waits for them, and re-layouts  5.34 us

profile of v1, /device:TPU:2, one launch (start us, length us, event | category | flops | bytes accessed | tf_op | source)
XLA Modules:
  0.0 202.5 jit_solution(6358404522864786990)
XLA Ops:
  0.6 1.3 copy.12.slots
  1.9 196.5 %shard_map.113 = (bf16[2,128,1408]{2,1,0:T(8,128)(2,1)}, bf16[2,128,1408]{2,1,0:T(8,128)(2,1)}) custom-call(bf16[128,1408]{1,0:T(8,128)(2,1)} %bitcast.18, bf16[128,1408]{1,0:T(8,128)(2,1)} %bitcast.19, bf16[3,128,1408]{2,1,0:T(8,128)(2,1)} %bitcast.13, bf16[8,128,1408]{2,1,0:T(8,128)(2,1)} %queue_in.1, s32[8]{0:T(128)} %entry.1, s32[2,1]{1,0:T(2,128)} %copy.12.slots, ...), custom_call_target="tpu_custom_call" | custom-call | tf_op jit(solution)/shard_map/pallas_call | solution.py:523
  198.4 2.0 copy.17
  200.5 2.0 copy.18

commit v2 on v1

--- a/solution.py
+++ b/solution.py
@@ -113,7 +113,7 @@
     x_in, up_in, bank_in, queue_in, entry, slots, qkv_in, out_in, skip_in, gains,
     desc_ref, asc_ref,
     xs, down, bank, queue, stage_qkv, act, wqv, wk, qt, kk, vt, qs, ks, vs, scores, ot, mt,
-    wo, wsk, part_send, part_recv, x1, operand, give, asc_send, asc_recv, asc_out,
+    wo, wsk, part_send, part_recv, x1, operand, give, asc_send, asc_recv, asc_out, own_up,
     load, store, act_send, act_recv, wo_send, wo_recv, wsk_send, wsk_recv,
     pair_send, pair_recv, w_send, w_recv, head_send, head_recv,
     part_ss, part_rs, down_ss, down_rs, give_ss, give_rs, rise_ss, rise_rs, mix_ss, mix_rs,
@@ -148,17 +148,37 @@
     for peer in greet:
         pl.semaphore_signal(barrier, inc=1, device_id=peer, device_id_type=MESH)
 
-    wo[0, HEAD:HP, :] = jnp.zeros((HP - HEAD, D), BF)
+    pad = HP - HEAD
+    wo[:, HEAD:HP, :] = jnp.zeros((RING, pad, D), BF)
+    for block in range(4):
+        wqv[block * HP + HEAD : (block + 1) * HP, :] = jnp.zeros((pad, D), BF)
     for block in range(2):
-        wqv[block * HP + HEAD : (block + 1) * HP, :] = jnp.zeros((HP - HEAD, D), BF)
-    wk[HEAD:128, :] = jnp.zeros((128 - HEAD, D), BF)
-    wk[128 + HP : 256, :] = jnp.zeros((128 - HP, D), BF)
-    qt[:, :, HP:128, :] = jnp.zeros((2, RING, 128 - HP, 256), BF)
+        wk[block * 128 + HEAD : (block + 1) * 128, :] = jnp.zeros((128 - HEAD, D), BF)
+    qt[:, :, HEAD:128, :] = jnp.zeros((2, 2, 128 - HEAD, 1024), BF)
+    mt[:, :, :, HEAD:HP, :] = jnp.zeros((2, 2, RING, pad, TOK), BF)
+    ones = (lax.broadcasted_iota(jnp.int32, (pad, 2048), 0) == 0).astype(F32).astype(BF)
+    for t in range(2):
+        vt[t, HEAD:HP, :] = ones
 
     gain_down, gain_up = gains[0:1, :], gains[1:2, :]
     loads[0].wait()
     act[0, 0] = layer_norm(xs[0].astype(F32), gain_down).astype(BF)
-    pl.semaphore_wait(barrier, len(greet))
+    loads[1].wait()
+    wqv[0:HEAD, :] = stage_qkv[0]
+    wqv[HP : HP + HEAD, :] = stage_qkv[2]
+    wk[0:HEAD, :] = stage_qkv[1]
+    loads[4].wait()
+    loads[5].wait()
+    skip_first = bank[slots[0, 0]]
+    skip_second = bank[slots[0, 1]]
+    rising = xs[2]
+    operand[0, 0:TOK, :] = jnp.where(y == 0, rising, skip_first)
+    give[0] = jnp.where(y == 0, skip_first, rising)
+    give[1] = skip_second
+
+    @pl.when(y == 1)
+    def _():
+        operand[1, 0:TOK, :] = skip_second
 
     def act_ring(t):
         return slot_ring(
@@ -167,52 +187,37 @@
         )
 
     rings = [act_ring(0), act_ring(1)]
-    out_ring = slot_ring(peers, wo_send, wo_recv, lambda p, half: wo.at[p, pl.ds(half * 48, 48), :])
+    out_ring = slot_ring(peers, wo_send, wo_recv, lambda p, half: wo.at[p, pl.ds(half * 48, 40 if half else 48), :])
     skip_ring = row_ring(peers, wsk_send, wsk_recv, z, wsk)
-
-    rings[0].begin(0)
-    rings[0].begin(1)
 
     def to_partner(src, dst, send, recv):
         return pltpu.make_async_remote_copy(
             src, dst, send, recv, device_id={"ctx": partner}, device_id_type=MESH
         )
 
-    loads[1].wait()
-    wqv[0:HEAD, :] = stage_qkv[0]
-    wqv[HP : HP + HEAD, :] = stage_qkv[2]
-    wk[0:HEAD, :] = stage_qkv[1]
     w_copies = [
-        to_partner(wqv.at[pl.ds(0, 2 * HP), :], wqv.at[pl.ds(2 * HP, 2 * HP), :], w_send.at[0], w_recv.at[0]),
-        to_partner(wk.at[pl.ds(0, HP), :], wk.at[pl.ds(128, HP), :], w_send.at[1], w_recv.at[1]),
+        to_partner(wqv.at[pl.ds(0, HEAD), :], wqv.at[pl.ds(2 * HP, HEAD), :], w_send.at[0], w_recv.at[0]),
+        to_partner(wqv.at[pl.ds(HP, HEAD), :], wqv.at[pl.ds(3 * HP, HEAD), :], w_send.at[1], w_recv.at[1]),
+        to_partner(wk.at[pl.ds(0, HEAD), :], wk.at[pl.ds(128, HEAD), :], w_send.at[2], w_recv.at[2]),
     ]
-    for copy in w_copies:
-        copy.start()
-
-    loads[4].wait()
-    loads[5].wait()
-    skip_first = bank[slots[0, 0]]
-    skip_second = bank[slots[1, 0]]
-    rising = xs[2]
-    operand[0, 0:TOK, :] = jnp.where(y == 0, rising, skip_first)
-    give[0] = jnp.where(y == 0, skip_first, rising)
-    give[1] = skip_second
     give_copies = [
         to_partner(give.at[t], operand.at[t, pl.ds(TOK, TOK), :], give_ss.at[t], give_rs.at[t])
         for t in range(2)
     ]
 
-    @pl.when(y == 1)
-    def _():
-        operand[1, 0:TOK, :] = skip_second
+    pl.semaphore_wait(barrier, len(greet))
+    rings[0].begin(0)
+    rings[0].begin(1)
+    for copy in w_copies:
+        copy.start()
 
     def pair_copies(t, g):
         lo, hi = GROUPS[g]
         n = (hi - lo) * TOK
         return [
             to_partner(
-                qs.at[t, pl.ds(lo, hi - lo)],
-                qt.at[t, pl.ds(lo, hi - lo), pl.ds(0, HP), pl.ds(128, 128)],
+                qs.at[t, :, pl.ds(lo * TOK, n)],
+                qt.at[t, 1, pl.ds(0, HEAD), pl.ds(lo * TOK, n)],
                 pair_send.at[t, g, 0], pair_recv.at[t, g, 0],
             ),
             to_partner(
@@ -222,7 +227,7 @@
             ),
             to_partner(
                 vs.at[t, :, pl.ds(lo * TOK, n)],
-                vt.at[t, :, pl.ds(1024 + lo * TOK, n)],
+                vt.at[t, pl.ds(0, HEAD), pl.ds(1024 + lo * TOK, n)],
                 pair_send.at[t, g, 2], pair_recv.at[t, g, 2],
             ),
         ]
@@ -233,29 +238,25 @@
         tokens = act[t, lo:hi].reshape(n, D)
         made = nt(wqv[...], tokens)
         keys = nt(tokens, wk[...]).astype(BF)
-        one = lax.broadcasted_iota(jnp.int32, (HP, n), 0) == HEAD
-        own_v = jnp.where(one, 1.0, made[HP : 2 * HP]).astype(BF)
-        pair_v = jnp.where(one, 1.0, made[3 * HP : 4 * HP]).astype(BF)
         made = made.astype(BF)
-        for p in range(lo, hi):
-            cols = slice((p - lo) * TOK, (p - lo + 1) * TOK)
-            qt[t, p, 0:HP, 0:128] = made[0:HP, cols]
-            qs[t, p] = made[2 * HP : 3 * HP, cols]
-        vt[t, :, lo * TOK : hi * TOK] = own_v
-        vs[t, :, lo * TOK : hi * TOK] = pair_v
+        qt[t, 0, 0:HEAD, lo * TOK : hi * TOK] = made[0:HEAD]
+        vt[t, 0:HEAD, lo * TOK : hi * TOK] = made[HP : HP + HEAD]
+        qs[t, :, lo * TOK : hi * TOK] = made[2 * HP : 2 * HP + HEAD]
+        vs[t, :, lo * TOK : hi * TOK] = made[3 * HP : 3 * HP + HEAD]
         kk[t, lo * TOK : hi * TOK, :] = keys[:, 0:128]
         ks[t, lo * TOK : hi * TOK, :] = keys[:, 128:256]
         for copy in pair_copies(t, g):
             copy.start()
 
-    def head_copy(t, p, mirror, delta):
+    def head_copy(t, half, p, mirror, delta):
         return pltpu.make_async_remote_copy(
-            ot.at[t, p], mt.at[t, mirror], head_send.at[t, p], head_recv.at[t, mirror],
+            ot.at[t, half, p], mt.at[t, half, mirror, pl.ds(0, HEAD), :],
+            head_send.at[t, half, p], head_recv.at[t, half, mirror],
             device_id={"ctx": y * 8 + (z + delta + 8) % 8}, device_id_type=MESH,
         )
 
-    def attend_block(t, p):
-        queries = qt[t, p]
+    def attend_block(t, half, b):
+        queries = qt[t, half, :, pl.ds(pl.multiple_of(b * 256, 256), 256)]
         peak = None
         for kb in range(8):
             made = jnp.dot(kk[t, kb * 256 : (kb + 1) * 256, :], queries, preferred_element_type=F32)
@@ -267,19 +268,19 @@
         for kb in range(8):
             powers = jnp.exp2((scores[kb] - peak) * (SCALE * LOG2E)).astype(BF)
             total += jnp.dot(vt[t, :, kb * 256 : (kb + 1) * 256], powers, preferred_element_type=F32)
-        return (total * (1.0 / total[HEAD : HEAD + 1, :])).astype(BF)
-
-    def attend(t, between):
+        return (total[0:HEAD] * (1.0 / total[HEAD : HEAD + 1, :])).astype(BF)
+
+    def attend(t, half, first, stop, between):
         def body(i, carry):
-            p = 7 - i
-            ot[t, p] = attend_block(t, p)
-            odd = p % 2
-            delta = ((p + 1) // 2) * (2 * odd - 1)
-            mirror = p + (2 * odd - 1) * (1 - p // 7)
-
-            @pl.when(p > 0)
+            b = 3 - i
+            made = attend_block(t, half, b)
+            ot[t, half, 2 * b + 1] = made[:, TOK : 2 * TOK]
+            ot[t, half, 2 * b] = made[:, 0:TOK]
+            head_copy(t, half, 2 * b + 1, 2 * b + 2 - b // 3, b + 1).start()
+
+            @pl.when(b > 0)
             def _():
-                head_copy(t, p, mirror, delta).start()
+                head_copy(t, half, 2 * b, 2 * b - 1, -b).start()
 
             for at, work in between.items():
 
@@ -289,26 +290,34 @@
 
             return carry
 
-        lax.fori_loop(0, 8, body, 0)
-        mt[t, 0] = ot[t, 0]
-
-    def out_project(t):
+        lax.fori_loop(first, stop, body, 0)
+        if stop == 4:
+            mt[t, half, 0, 0:HEAD, :] = ot[t, half, 0]
+
+    def part_copy(t, h):
+        return to_partner(
+            part_send.at[t, pl.ds(h * 64, 64), :], part_recv.at[t, pl.ds(h * 64, 64), :],
+            part_ss.at[t, h], part_rs.at[t, h],
+        )
+
+    def heads_times_out(t, half):
         for p in range(1, 8):
-            head_copy(t, p, p, 0).wait_recv()
+            head_copy(t, half, p, p, 1).wait_recv()
         weights = wo[...].reshape(RING * HP, D)
-        heads = mt[t].reshape(RING * HP, 256)
-        part_send[t] = tn(heads[:, 128:256], weights).astype(BF)
-        copies = [
-            to_partner(
-                part_send.at[t, pl.ds(h * 64, 64), :], part_recv.at[t, pl.ds(h * 64, 64), :],
-                part_ss.at[t, h], part_rs.at[t, h],
-            )
-            for h in range(2)
-        ]
-        for copy in copies:
-            copy.start()
-        own = tn(heads[:, 0:128], weights) + xs[t].astype(F32)
-        return own, copies
+        return tn(mt[t, half].reshape(RING * HP, TOK), weights)
+
+    def project_pair(t):
+        part_send[t] = heads_times_out(t, 1).astype(BF)
+        for h in range(2):
+            part_copy(t, h).start()
+
+    def project_own(t):
+        return heads_times_out(t, 0) + xs[t].astype(F32)
+
+    def finish(t, h, own):
+        rows = slice(h * 64, (h + 1) * 64)
+        part_copy(t, h).wait_recv()
+        x1[t, rows, :] = (own[rows] + part_recv[t, rows, :].astype(F32)).astype(BF)
 
     def down_copy(h):
         return pltpu.make_async_remote_copy(
@@ -333,48 +342,46 @@
 
     def ascend_first(t):
         asc_send[t] = jnp.dot(operand[t, TOK : 2 * TOK, :], wsk[...], preferred_element_type=F32).astype(BF)
-        mix_copy(t).start()
-        return jnp.dot(operand[t, 0:TOK, :], wsk[...], preferred_element_type=F32)
-
-    def ascend_last(t, own):
+        own_up[...] = jnp.dot(operand[t, 0:TOK, :], wsk[...], preferred_element_type=F32)
+
+    def ascend_last(t):
         mix_copy(t).wait_recv()
-        asc_out[t] = layer_norm(own + asc_recv[t].astype(F32), gain_up).astype(BF)
+        asc_out[t] = layer_norm(own_up[...] + asc_recv[t].astype(F32), gain_up).astype(BF)
         pltpu.make_async_copy(asc_out.at[t], asc_ref.at[t], store.at[1, t]).start()
 
-    for j in range(7):
+    for j in range(4):
         rings[0].step(j)
-        if j == 1:
-            for copy in w_copies:
-                copy.wait_recv()
-            project(0, 0)
-            project(0, 1)
-            give_copies[0].start()
-            pl.when(y == 0)(lambda: give_copies[1].start())
-        if j == 3:
-            project(0, 2)
-        if j == 5:
-            loads[2].wait()
-            out_ring.begin(0)
-            out_ring.begin(1)
-            project(0, 3)
-        if j == 6:
-            project(0, 4)
+    for copy in w_copies:
+        copy.wait_recv()
+    for g in range(3):
+        project(0, g)
+    rings[0].step(4)
+    rings[0].step(5)
+    loads[2].wait()
+    out_ring.begin(0)
+    project(0, 3)
+    rings[0].step(6)
+    out_ring.begin(1)
+    project(0, 4)
     for g in range(5):
         for copy in pair_copies(0, g):
             copy.wait_recv()
-    attend(0, {1: lambda: out_ring.step(0), 3: lambda: out_ring.step(1), 5: lambda: out_ring.step(2), 7: lambda: out_ring.step(3)})
-    for j in range(4, 7):
-        out_ring.step(j)
+    give_copies[0].start()
+    pl.when(y == 0)(lambda: give_copies[1].start())
+    attend(0, 1, 0, 4, {1: lambda: out_ring.step(0), 3: lambda: out_ring.step(1)})
+    attend(0, 0, 0, 4, {1: lambda: out_ring.step(2), 3: lambda: out_ring.step(3)})
     loads[3].wait()
+    out_ring.step(4)
+    out_ring.step(5)
     skip_ring.begin(0)
+    out_ring.step(6)
     skip_ring.begin(1)
-    own, copies = out_project(0)
+    project_pair(0)
+    own = project_own(0)
     skip_ring.step(0)
     skip_ring.step(1)
     for h in range(2):
-        rows = slice(h * 64, (h + 1) * 64)
-        copies[h].wait_recv()
-        x1[0, rows, :] = (own[rows] + part_recv[0, rows, :].astype(F32)).astype(BF)
+        finish(0, h, own)
         down_copy(h).start()
     pltpu.make_async_copy(x1.at[0], desc_ref.at[0], store.at[0, 0]).start()
 
@@ -388,6 +395,8 @@
     def _():
         turn_copy().start()
 
+    skip_ring.step(2)
+    skip_ring.step(3)
     loads[6].wait()
     entering = queue[entry[0]]
     for h in range(2):
@@ -395,42 +404,33 @@
         down_copy(h).wait_recv()
         xs[1, rows, :] = jnp.where(s == 0, entering[rows], down[rows, :])
         act[1, 0, rows, :] = layer_norm(xs[1, rows, :].astype(F32), gain_down).astype(BF)
-        rings[1].begin(h)
     project(1, 0)
-    skip_ring.step(2)
-    skip_ring.step(3)
-    for j in range(7):
-        rings[1].step(j)
-        if j == 1:
-            project(1, 1)
-            skip_ring.step(4)
-        if j == 3:
-            project(1, 2)
-            skip_ring.step(5)
-        if j == 5:
-            project(1, 3)
-            skip_ring.step(6)
-        if j == 6:
-            project(1, 4)
+    skip_ring.step(4)
+    rings[1].begin(0)
+    skip_ring.step(5)
+    rings[1].begin(1)
+    skip_ring.step(6)
 
     give_copies[0].wait_recv()
-    own_up = ascend_first(0)
-    for g in range(5):
-        for copy in pair_copies(1, g):
-            copy.wait_recv()
-    ascend_last(0, own_up)
-
-    @pl.when(s > 0)
-    def _():
-        rise_copy().start()
-
-    attend(1, {})
-
-    own, copies = out_project(1)
+    ascend_first(0)
+    mix_copy(0).start()
+    rings[1].step(0)
+    rings[1].step(1)
+    project(1, 1)
+    ascend_last(0)
+    pl.when(s > 0)(lambda: rise_copy().start())
+    rings[1].step(2)
+    rings[1].step(3)
+    project(1, 2)
 
     @pl.when(y == 1)
     def _():
         give_copies[1].wait_recv()
+        ascend_first(1)
+
+    rings[1].step(4)
+    rings[1].step(5)
+    project(1, 3)
 
     @pl.when(jnp.logical_and(y == 0, s < SEGS - 1))
     def _():
@@ -442,14 +442,23 @@
     @pl.when(y == 0)
     def _():
         turn_copy().wait_recv()
-
-    own_up = ascend_first(1)
+        ascend_first(1)
+
+    rings[1].step(6)
+    project(1, 4)
+    for g in range(5):
+        for copy in pair_copies(1, g):
+            copy.wait_recv()
+    mix_copy(1).start()
+    attend(1, 1, 0, 4, {})
+    attend(1, 0, 0, 2, {})
+    project_pair(1)
+    attend(1, 0, 2, 4, {})
+    ascend_last(1)
+    own = project_own(1)
     for h in range(2):
-        rows = slice(h * 64, (h + 1) * 64)
-        copies[h].wait_recv()
-        x1[1, rows, :] = (own[rows] + part_recv[1, rows, :].astype(F32)).astype(BF)
+        finish(1, h, own)
     pltpu.make_async_copy(x1.at[1], desc_ref.at[1], store.at[0, 1]).start()
-    ascend_last(1, own_up)
 
     for ring in (*rings, out_ring, skip_ring):
         ring.drain()
@@ -461,14 +470,12 @@
         for g in range(5):
             for copy in pair_copies(t, g):
                 copy.wait_send()
-        for p in range(1, 8):
-            head_copy(t, p, p, 0).wait_send()
+        mix_copy(t).wait_send()
+        for half in range(2):
+            for p in range(1, 8):
+                head_copy(t, half, p, p, 1).wait_send()
         for h in range(2):
-            to_partner(
-                part_send.at[t, pl.ds(h * 64, 64), :], part_recv.at[t, pl.ds(h * 64, 64), :],
-                part_ss.at[t, h], part_rs.at[t, h],
-            ).wait_send()
-        mix_copy(t).wait_send()
+            part_copy(t, h).wait_send()
     for h in range(2):
         down_copy(h).wait_send()
     pl.when(s > 0)(lambda: rise_copy().wait_send())
@@ -495,15 +502,15 @@
         V((2, RING, TOK, D), BF),
         V((4 * HP, D), BF),
         V((256, D), BF),
-        V((2, RING, 128, 256), BF),
+        V((2, 2, 128, 1024), BF),
         V((2, 2048, 128), BF),
         V((2, HP, 2048), BF),
-        V((2, RING, HP, 128), BF),
+        V((2, HEAD, 1024), BF),
         V((2, 1024, 128), BF),
-        V((2, HP, 1024), BF),
+        V((2, HEAD, 1024), BF),
         V((8, 256, 256), F32),
-        V((2, RING, HP, 256), BF),
-        V((2, RING, HP, 256), BF),
+        V((2, 2, RING, HEAD, TOK), BF),
+        V((2, 2, RING, HP, TOK), BF),
         V((RING, HP, D), BF),
         V((D, D), BF),
         V((2, TOK, D), BF),
@@ -514,9 +521,10 @@
         V((2, TOK, D), BF),
         V((2, TOK, D), BF),
         V((2, TOK, D), BF),
+        V((TOK, D), F32),
         dma((7,)), dma((2, 2)),
         dma((2, 2, 7)), dma((2, 2, 7)), dma((2, 7)), dma((2, 7)), dma((2, 7)), dma((2, 7)),
-        dma((2, 5, 3)), dma((2, 5, 3)), dma((2,)), dma((2,)), dma((2, 8)), dma((2, 8)),
+        dma((2, 5, 3)), dma((2, 5, 3)), dma((3,)), dma((3,)), dma((2, 2, 8)), dma((2, 2, 8)),
         dma((2, 2)), dma((2, 2)), dma((2,)), dma((2,)), dma((2,)), dma((2,)),
         dma((2,)), dma((2,)), dma((2,)), dma((2,)),
     ]
@@ -533,7 +541,7 @@
             collective_id=0, has_side_effects=True, vmem_limit_bytes=60 * 1024 * 1024
         ),
     )(
-        carried_down[0], carried_up[0], skip_bank[0], queue, next_entry, skip_slot,
+        carried_down[0], carried_up[0], skip_bank[0], queue, next_entry, skip_slot.T,
         w_qkv[0], w_out[0], w_skip[0], gains[0],
     )
     return desc[:, None], asc[:, None]

time: 206 us -> 173 us (0.84); the launches traced: 202 us -> 173 us
  Pallas kernels: 196 us -> 168 us
    pallas_call x1, Pallas kernels: 196 us -> 168 us  [on_device(): pl.pallas_call(kernel, out_shape=(jax.ShapeDtypeStruct((2, TOK, D), BF),...]
    unnamed x3 -> x2, local copies, waits for them, and re-layouts: 5.34 us -> 4.04 us
where the time goes in v2:
time: 173 us
  Pallas kernels  168 us (97%)
  local copies, waits for them, and re-layouts  4.04 us (2%)
    pallas_call x1, Pallas kernels, on_device(): pl.pallas_call(kernel, out_shape=(jax.ShapeDtypeStruct((2, TOK, D), BF),...  168 us
    unnamed x2, local copies, waits for them, and re-layouts  4.04 us

profile of v2, /device:TPU:2, one launch (start us, length us, event | category | flops | bytes accessed | tf_op | source)
XLA Modules:
  0.0 172.6 jit_solution(13458306726235146676)
XLA Ops:
  0.6 167.9 %shard_map.113 = (bf16[2,128,1408]{2,1,0:T(8,128)(2,1)}, bf16[2,128,1408]{2,1,0:T(8,128)(2,1)}) custom-call(bf16[128,1408]{1,0:T(8,128)(2,1)} %bitcast.19, bf16[128,1408]{1,0:T(8,128)(2,1)} %bitcast.20, bf16[3,128,1408]{2,1,0:T(8,128)(2,1)} %bitcast.14, bf16[8,128,1408]{2,1,0:T(8,128)(2,1)} %queue_in.1, s32[8]{0:T(128)} %entry.1, s32[1,2]{1,0:T(1,128)} %bitcast.23, ...), custom_call_target="tpu_custom_call" | custom-call | tf_op jit(solution)/shard_map/pallas_call | solution.py:531
  168.5 2.0 %copy.16 = bf16[2,1,128,1408]{3,2,1,0:T(8,128)(2,1)} copy(bf16[2,1,128,1408]{3,2,1,0:T(8,128)(2,1)} %bitcast.17) | data formatting | bytes 1441792
  170.6 2.0 %copy.17 = bf16[2,1,128,1408]{3,2,1,0:T(8,128)(2,1)} copy(bf16[2,1,128,1408]{3,2,1,0:T(8,128)(2,1)} %bitcast.16) | data formatting | bytes 1441792

commit v3 on v2

--- a/solution.py
+++ b/solution.py
@@ -417,11 +417,11 @@
     rings[1].step(0)
     rings[1].step(1)
     project(1, 1)
-    ascend_last(0)
-    pl.when(s > 0)(lambda: rise_copy().start())
     rings[1].step(2)
     rings[1].step(3)
     project(1, 2)
+    ascend_last(0)
+    pl.when(s > 0)(lambda: rise_copy().start())
 
     @pl.when(y == 1)
     def _():
@@ -431,6 +431,8 @@
     rings[1].step(4)
     rings[1].step(5)
     project(1, 3)
+    rings[1].step(6)
+    project(1, 4)
 
     @pl.when(jnp.logical_and(y == 0, s < SEGS - 1))
     def _():
@@ -444,8 +446,6 @@
         turn_copy().wait_recv()
         ascend_first(1)
 
-    rings[1].step(6)
-    project(1, 4)
     for g in range(5):
         for copy in pair_copies(1, g):
             copy.wait_recv()
@@ -483,6 +483,27 @@
     for t in range(2):
         pltpu.make_async_copy(x1.at[t], desc_ref.at[t], store.at[0, t]).wait()
         pltpu.make_async_copy(asc_out.at[t], asc_ref.at[t], store.at[1, t]).wait()
+
+
+def hand_on(desc_in, asc_in, desc_ref, asc_ref, held, read, write):
+    ends = ((desc_in, desc_ref), (asc_in, asc_ref))
+    pieces = [(a, t, h) for t in range(2) for a in range(2) for h in range(2)]
+
+    def fetch(a, t, h):
+        rows = pl.ds(h * 64, 64)
+        return pltpu.make_async_copy(ends[a][0].at[t, rows, :], held.at[a, t, rows, :], read.at[a, t, h])
+
+    def put(a, t, h):
+        rows = pl.ds(h * 64, 64)
+        return pltpu.make_async_copy(held.at[a, t, rows, :], ends[a][1].at[t, rows, :], write.at[a, t, h])
+
+    for piece in pieces:
+        fetch(*piece).start()
+    for piece in pieces:
+        fetch(*piece).wait()
+        put(*piece).start()
+    for piece in pieces:
+        put(*piece).wait()
 
 
 def on_device(
@@ -544,6 +565,17 @@
         carried_down[0], carried_up[0], skip_bank[0], queue, next_entry, skip_slot.T,
         w_qkv[0], w_out[0], w_skip[0], gains[0],
     )
+    desc, asc = pl.pallas_call(
+        hand_on,
+        out_shape=(
+            jax.ShapeDtypeStruct((2, TOK, D), BF),
+            jax.ShapeDtypeStruct((2, TOK, D), BF),
+        ),
+        in_specs=[hbm, hbm],
+        out_specs=(hbm, hbm),
+        scratch_shapes=[V((2, 2, TOK, D), BF), dma((2, 2, 2)), dma((2, 2, 2))],
+        compiler_params=pltpu.CompilerParams(vmem_limit_bytes=60 * 1024 * 1024),
+    )(desc, asc)
     return desc[:, None], asc[:, None]
 
 

time: 173 us -> 167 us (0.965)
  local copies, waits for them, and re-layouts: 4.04 us -> 0 us
  Pallas kernels: 168 us -> 164 us
    pallas_call x1, Pallas kernels: 168 us -> 162 us  [on_device(): pl.pallas_call(kernel, out_shape=(jax.ShapeDtypeStruct((2, TOK, D), BF),...]
    unnamed x2 -> x0, local copies, waits for them, and re-layouts: 4.04 us -> none
    pallas_call x0 -> x1, Pallas kernels: none -> 2.24 us  [on_device(): pl.pallas_call(hand_on, out_shape=(jax.ShapeDtypeStruct((2, TOK, D), BF),...]
where the time goes in v3:
time: 167 us; the launch traced here: 165 us
  Pallas kernels  164 us (98%)
    pallas_call x1, Pallas kernels, on_device(): pl.pallas_call(kernel, out_shape=(jax.ShapeDtypeStruct((2, TOK, D), BF),...  162 us

profile of v3, /device:TPU:2, one launch (start us, length us, event | category | flops | bytes accessed | tf_op | source)
XLA Modules:
  0.0 165.0 jit_solution(5846384989706063991)
XLA Ops:
  0.6 162.0 %shard_map.113 = (bf16[2,128,1408]{2,1,0:T(8,128)(2,1)}, bf16[2,128,1408]{2,1,0:T(8,128)(2,1)}) custom-call(bf16[128,1408]{1,0:T(8,128)(2,1)} %bitcast.17, bf16[128,1408]{1,0:T(8,128)(2,1)} %bitcast.18, bf16[3,128,1408]{2,1,0:T(8,128)(2,1)} %bitcast.14, bf16[8,128,1408]{2,1,0:T(8,128)(2,1)} %queue_in.1, s32[8]{0:T(128)} %entry.1, s32[1,2]{1,0:T(1,128)} %bitcast.21, ...), custom_call_target="tpu_custom_call" | custom-call | tf_op jit(solution)/shard_map/pallas_call | solution.py:552
  162.6 2.2 %shard_map.114 = (bf16[2,128,1408]{2,1,0:T(8,128)(2,1)}, bf16[2,128,1408]{2,1,0:T(8,128)(2,1)}) custom-call(bf16[2,128,1408]{2,1,0:T(8,128)(2,1)} %get-tuple-element.6.desc_in, bf16[2,128,1408]{2,1,0:T(8,128)(2,1)} %get-tuple-element.7.asc_in), custom_call_target="tpu_custom_call" | custom-call | tf_op jit(solution)/shard_map/pallas_call | solution.py:568

commit v4 on v3

--- a/solution.py
+++ b/solution.py
@@ -18,6 +18,7 @@
 BF = jnp.bfloat16
 F32 = jnp.float32
 GROUPS = ((0, 1), (1, 3), (3, 5), (5, 7), (7, 8))
+EARLY = tuple((ring + start, size) for ring in (0, 1024) for start, size in ((0, 256), (256, 256), (512, 256), (768, 128)))
 
 
 def slot_of(delta):
@@ -113,10 +114,10 @@
     x_in, up_in, bank_in, queue_in, entry, slots, qkv_in, out_in, skip_in, gains,
     desc_ref, asc_ref,
     xs, down, bank, queue, stage_qkv, act, wqv, wk, qt, kk, vt, qs, ks, vs, scores, ot, mt,
-    wo, wsk, part_send, part_recv, x1, operand, give, asc_send, asc_recv, asc_out, own_up,
+    wo, wsk, part_send, part_recv, x1, operand, give, asc_send, asc_recv, asc_out, own_up, early_peak, early_total,
     load, store, act_send, act_recv, wo_send, wo_recv, wsk_send, wsk_recv,
     pair_send, pair_recv, w_send, w_recv, head_send, head_recv,
-    part_ss, part_rs, down_ss, down_rs, give_ss, give_rs, rise_ss, rise_rs, mix_ss, mix_rs,
+    swap_send, swap_recv, part_ss, part_rs, down_ss, down_rs, give_ss, give_rs, rise_ss, rise_rs, mix_ss, mix_rs,
 ):
     s = lax.axis_index("segment")
     c = lax.axis_index("ctx")
@@ -143,13 +144,13 @@
 
     barrier = pltpu.get_barrier_semaphore()
     diagonal = {"segment": (s + SEGS + 1 - 2 * y) % SEGS, "ctx": partner}
-    greet = [{"ctx": ring_peer(d)} for d in (1, -1, 2, -2, 3, -3, 4)]
+    greet = [{"ctx": ring_peer(d)} for d in (1, -1)]
     greet += [{"ctx": partner}, {"segment": above}, {"segment": below}, diagonal]
     for peer in greet:
         pl.semaphore_signal(barrier, inc=1, device_id=peer, device_id_type=MESH)
 
     pad = HP - HEAD
-    wo[:, HEAD:HP, :] = jnp.zeros((RING, pad, D), BF)
+    wo[:, HEAD:HP, :] = jnp.zeros((2 * RING, pad, D), BF)
     for block in range(4):
         wqv[block * HP + HEAD : (block + 1) * HP, :] = jnp.zeros((pad, D), BF)
     for block in range(2):
@@ -238,10 +239,12 @@
         tokens = act[t, lo:hi].reshape(n, D)
         made = nt(wqv[...], tokens)
         keys = nt(tokens, wk[...]).astype(BF)
+        own_q = (made[0:HEAD] * (SCALE * LOG2E)).astype(BF)
+        pair_q = (made[2 * HP : 2 * HP + HEAD] * (SCALE * LOG2E)).astype(BF)
         made = made.astype(BF)
-        qt[t, 0, 0:HEAD, lo * TOK : hi * TOK] = made[0:HEAD]
+        qt[t, 0, 0:HEAD, lo * TOK : hi * TOK] = own_q
         vt[t, 0:HEAD, lo * TOK : hi * TOK] = made[HP : HP + HEAD]
-        qs[t, :, lo * TOK : hi * TOK] = made[2 * HP : 2 * HP + HEAD]
+        qs[t, :, lo * TOK : hi * TOK] = pair_q
         vs[t, :, lo * TOK : hi * TOK] = made[3 * HP : 3 * HP + HEAD]
         kk[t, lo * TOK : hi * TOK, :] = keys[:, 0:128]
         ks[t, lo * TOK : hi * TOK, :] = keys[:, 128:256]
@@ -249,10 +252,16 @@
             copy.start()
 
     def head_copy(t, half, p, mirror, delta):
+        ring = 1 - y if t == 1 and half == 1 else y
         return pltpu.make_async_remote_copy(
             ot.at[t, half, p], mt.at[t, half, mirror, pl.ds(0, HEAD), :],
             head_send.at[t, half, p], head_recv.at[t, half, mirror],
-            device_id={"ctx": y * 8 + (z + delta + 8) % 8}, device_id_type=MESH,
+            device_id={"ctx": ring * 8 + (z + delta + 8) % 8}, device_id_type=MESH,
+        )
+
+    def swap_copy(p):
+        return to_partner(
+            wo.at[p, pl.ds(0, HEAD), :], wo.at[RING + p, pl.ds(0, HEAD), :], swap_send.at[p], swap_recv.at[p]
         )
 
     def attend_block(t, half, b):
@@ -266,22 +275,51 @@
         peak = jnp.max(peak, axis=0, keepdims=True)
         total = jnp.zeros((HP, 256), F32)
         for kb in range(8):
-            powers = jnp.exp2((scores[kb] - peak) * (SCALE * LOG2E)).astype(BF)
+            powers = jnp.exp2(scores[kb] - peak).astype(BF)
             total += jnp.dot(vt[t, :, kb * 256 : (kb + 1) * 256], powers, preferred_element_type=F32)
         return (total[0:HEAD] * (1.0 / total[HEAD : HEAD + 1, :])).astype(BF)
 
-    def attend(t, half, first, stop, between):
+    def attend_early(b):
+        queries = qt[1, 1, :, pl.ds(pl.multiple_of(b * 256, 256), 256)]
+        peak = None
+        for kb, (start, size) in enumerate(EARLY):
+            made = jnp.dot(kk[1, start : start + size, :], queries, preferred_element_type=F32)
+            scores[kb, 0:size, :] = made
+            top = jnp.max(made.reshape(size // 8, 8, 256), axis=0)
+            peak = top if peak is None else jnp.maximum(peak, top)
+        peak = jnp.max(peak, axis=0, keepdims=True)
+        total = jnp.zeros((HP, 256), F32)
+        for kb, (start, size) in enumerate(EARLY):
+            powers = jnp.exp2(scores[kb, 0:size, :] - peak).astype(BF)
+            total += jnp.dot(vt[1, :, start : start + size], powers, preferred_element_type=F32)
+        early_peak[b] = jnp.broadcast_to(peak, (8, 256))
+        early_total[b] = total
+
+    def attend_late(b):
+        queries = qt[1, 1, :, pl.ds(pl.multiple_of(b * 256, 256), 256)]
+        keys = jnp.concatenate([kk[1, 896:1024, :], kk[1, 1920:2048, :]], axis=0)
+        values = jnp.concatenate([vt[1, :, 896:1024], vt[1, :, 1920:2048]], axis=1)
+        made = jnp.dot(keys, queries, preferred_element_type=F32)
+        before = early_peak[b][0:1, :]
+        peak = jnp.maximum(before, jnp.max(jnp.max(made.reshape(32, 8, 256), axis=0), axis=0, keepdims=True))
+        powers = jnp.exp2(made - peak).astype(BF)
+        total = early_total[b] * jnp.exp2(before - peak)
+        total += jnp.dot(values, powers, preferred_element_type=F32)
+        return (total[0:HEAD] * (1.0 / total[HEAD : HEAD + 1, :])).astype(BF)
+
+    def pass_on(t, half, b, made):
+        ot[t, half, 2 * b + 1] = made[:, TOK : 2 * TOK]
+        ot[t, half, 2 * b] = made[:, 0:TOK]
+        head_copy(t, half, 2 * b + 1, 2 * b + 2 - b // 3, b + 1).start()
+
+        @pl.when(b > 0)
+        def _():
+            head_copy(t, half, 2 * b, 2 * b - 1, -b).start()
+
+    def attend(t, half, first, stop, between, block=None):
         def body(i, carry):
             b = 3 - i
-            made = attend_block(t, half, b)
-            ot[t, half, 2 * b + 1] = made[:, TOK : 2 * TOK]
-            ot[t, half, 2 * b] = made[:, 0:TOK]
-            head_copy(t, half, 2 * b + 1, 2 * b + 2 - b // 3, b + 1).start()
-
-            @pl.when(b > 0)
-            def _():
-                head_copy(t, half, 2 * b, 2 * b - 1, -b).start()
-
+            pass_on(t, half, b, attend_block(t, half, b) if block is None else block(b))
             for at, work in between.items():
 
                 @pl.when(i == at)
@@ -291,33 +329,32 @@
             return carry
 
         lax.fori_loop(first, stop, body, 0)
-        if stop == 4:
+        if stop == 4 and t == 1 and half == 1:
+            head_copy(t, half, 0, 0, 0).start()
+        elif stop == 4:
             mt[t, half, 0, 0:HEAD, :] = ot[t, half, 0]
 
-    def part_copy(t, h):
+    def part_copy(h):
         return to_partner(
-            part_send.at[t, pl.ds(h * 64, 64), :], part_recv.at[t, pl.ds(h * 64, 64), :],
-            part_ss.at[t, h], part_rs.at[t, h],
-        )
-
-    def heads_times_out(t, half):
-        for p in range(1, 8):
+            part_send.at[pl.ds(h * 64, 64), :], part_recv.at[pl.ds(h * 64, 64), :],
+            part_ss.at[h], part_rs.at[h],
+        )
+
+    def heads_times_out(t, half, slots):
+        for p in range(1 if t == 0 or half == 0 else 0, 8):
             head_copy(t, half, p, p, 1).wait_recv()
-        weights = wo[...].reshape(RING * HP, D)
+        weights = wo[slots : slots + RING].reshape(RING * HP, D)
         return tn(mt[t, half].reshape(RING * HP, TOK), weights)
 
-    def project_pair(t):
-        part_send[t] = heads_times_out(t, 1).astype(BF)
+    def project_pair():
+        part_send[...] = heads_times_out(0, 1, 0).astype(BF)
         for h in range(2):
-            part_copy(t, h).start()
-
-    def project_own(t):
-        return heads_times_out(t, 0) + xs[t].astype(F32)
-
-    def finish(t, h, own):
+            part_copy(h).start()
+
+    def finish(h, own):
         rows = slice(h * 64, (h + 1) * 64)
-        part_copy(t, h).wait_recv()
-        x1[t, rows, :] = (own[rows] + part_recv[t, rows, :].astype(F32)).astype(BF)
+        part_copy(h).wait_recv()
+        x1[0, rows, :] = (own[rows] + part_recv[rows, :].astype(F32)).astype(BF)
 
     def down_copy(h):
         return pltpu.make_async_remote_copy(
@@ -366,23 +403,36 @@
     for g in range(5):
         for copy in pair_copies(0, g):
             copy.wait_recv()
-    give_copies[0].start()
-    pl.when(y == 0)(lambda: give_copies[1].start())
-    attend(0, 1, 0, 4, {1: lambda: out_ring.step(0), 3: lambda: out_ring.step(1)})
-    attend(0, 0, 0, 4, {1: lambda: out_ring.step(2), 3: lambda: out_ring.step(3)})
+    swap_copy(0).start()
+
+    def out_step(j):
+        def work():
+            out_ring.step(j)
+            if j % 2:
+                swap_copy(j).start()
+                swap_copy(j + 1).start()
+
+        return work
+
+    attend(0, 1, 0, 4, {1: out_step(0), 3: out_step(1)})
+    attend(0, 0, 0, 4, {1: out_step(2), 3: out_step(3)})
     loads[3].wait()
     out_ring.step(4)
     out_ring.step(5)
     skip_ring.begin(0)
     out_ring.step(6)
     skip_ring.begin(1)
-    project_pair(0)
-    own = project_own(0)
+    project_pair()
+    own = heads_times_out(0, 0, 0) + xs[0].astype(F32)
     skip_ring.step(0)
     skip_ring.step(1)
     for h in range(2):
-        finish(0, h, own)
+        finish(h, own)
         down_copy(h).start()
+    for p in range(5, 8):
+        swap_copy(p).start()
+    give_copies[0].start()
+    pl.when(y == 0)(lambda: give_copies[1].start())
     pltpu.make_async_copy(x1.at[0], desc_ref.at[0], store.at[0, 0]).start()
 
     last = s == SEGS - 1
@@ -446,19 +496,27 @@
         turn_copy().wait_recv()
         ascend_first(1)
 
-    for g in range(5):
+    for g in range(4):
         for copy in pair_copies(1, g):
             copy.wait_recv()
+
+    def early(i, carry):
+        attend_early(2 - i)
+        return carry
+
     mix_copy(1).start()
-    attend(1, 1, 0, 4, {})
-    attend(1, 0, 0, 2, {})
-    project_pair(1)
-    attend(1, 0, 2, 4, {})
+    lax.fori_loop(0, 3, early, 0)
+    for copy in pair_copies(1, 4):
+        copy.wait_recv()
+    attend(1, 1, 0, 1, {})
+    attend(1, 1, 1, 4, {}, attend_late)
+    attend(1, 0, 0, 4, {})
+    for p in range(8):
+        swap_copy(p).wait_recv()
+    own = heads_times_out(1, 1, RING) + xs[1].astype(F32)
+    x1[1] = (own + heads_times_out(1, 0, 0)).astype(BF)
+    pltpu.make_async_copy(x1.at[1], desc_ref.at[1], store.at[0, 1]).start()
     ascend_last(1)
-    own = project_own(1)
-    for h in range(2):
-        finish(1, h, own)
-    pltpu.make_async_copy(x1.at[1], desc_ref.at[1], store.at[0, 1]).start()
 
     for ring in (*rings, out_ring, skip_ring):
         ring.drain()
@@ -472,11 +530,12 @@
                 copy.wait_send()
         mix_copy(t).wait_send()
         for half in range(2):
-            for p in range(1, 8):
+            for p in range(1 if t == 0 or half == 0 else 0, 8):
                 head_copy(t, half, p, p, 1).wait_send()
-        for h in range(2):
-            part_copy(t, h).wait_send()
+    for p in range(8):
+        swap_copy(p).wait_send()
     for h in range(2):
+        part_copy(h).wait_send()
         down_copy(h).wait_send()
     pl.when(s > 0)(lambda: rise_copy().wait_send())
     pl.when(jnp.logical_and(last, y == 1))(lambda: turn_copy().wait_send())
@@ -532,10 +591,10 @@
         V((8, 256, 256), F32),
         V((2, 2, RING, HEAD, TOK), BF),
         V((2, 2, RING, HP, TOK), BF),
-        V((RING, HP, D), BF),
+        V((2 * RING, HP, D), BF),
         V((D, D), BF),
-        V((2, TOK, D), BF),
-        V((2, TOK, D), BF),
+        V((TOK, D), BF),
+        V((TOK, D), BF),
         V((2, TOK, D), BF),
         V((2, 2 * TOK, D), BF),
         V((2, TOK, D), BF),
@@ -543,10 +602,12 @@
         V((2, TOK, D), BF),
         V((2, TOK, D), BF),
         V((TOK, D), F32),
+        V((3, 8, 256), F32),
+        V((3, HP, 256), F32),
         dma((7,)), dma((2, 2)),
         dma((2, 2, 7)), dma((2, 2, 7)), dma((2, 7)), dma((2, 7)), dma((2, 7)), dma((2, 7)),
         dma((2, 5, 3)), dma((2, 5, 3)), dma((3,)), dma((3,)), dma((2, 2, 8)), dma((2, 2, 8)),
-        dma((2, 2)), dma((2, 2)), dma((2,)), dma((2,)), dma((2,)), dma((2,)),
+        dma((8,)), dma((8,)), dma((2,)), dma((2,)), dma((2,)), dma((2,)), dma((2,)), dma((2,)),
         dma((2,)), dma((2,)), dma((2,)), dma((2,)),
     ]
     desc, asc = pl.pallas_call(

time: 167 us -> 165 us (0.988)
  Pallas kernels: 164 us -> 162 us
    pallas_call x1, Pallas kernels: 162 us -> 160 us  [on_device(): pl.pallas_call(kernel, out_shape=(jax.ShapeDtypeStruct((2, TOK, D), BF),...]
where the time goes in v4:
time: 165 us; the launch traced here: 163 us
  Pallas kernels  162 us (98%)
    pallas_call x1, Pallas kernels, on_device(): pl.pallas_call(kernel, out_shape=(jax.ShapeDtypeStruct((2, TOK, D), BF),...  160 us

profile of v4, /device:TPU:2, one launch (start us, length us, event | category | flops | bytes accessed | tf_op | source)
XLA Modules:
  0.0 162.7 jit_solution(1306451215582393222)
XLA Ops:
  0.6 159.7 %shard_map.113 = (bf16[2,128,1408]{2,1,0:T(8,128)(2,1)}, bf16[2,128,1408]{2,1,0:T(8,128)(2,1)}) custom-call(bf16[128,1408]{1,0:T(8,128)(2,1)} %bitcast.17, bf16[128,1408]{1,0:T(8,128)(2,1)} %bitcast.18, bf16[3,128,1408]{2,1,0:T(8,128)(2,1)} %bitcast.14, bf16[8,128,1408]{2,1,0:T(8,128)(2,1)} %queue_in.1, s32[8]{0:T(128)} %entry.1, s32[1,2]{1,0:T(1,128)} %bitcast.21, ...), custom_call_target="tpu_custom_call" | custom-call | tf_op jit(solution)/shard_map/pallas_call | solution.py:613
  160.3 2.2 %shard_map.114 = (bf16[2,128,1408]{2,1,0:T(8,128)(2,1)}, bf16[2,128,1408]{2,1,0:T(8,128)(2,1)}) custom-call(bf16[2,128,1408]{2,1,0:T(8,128)(2,1)} %get-tuple-element.6.desc_in, bf16[2,128,1408]{2,1,0:T(8,128)(2,1)} %get-tuple-element.7.asc_in), custom_call_target="tpu_custom_call" | custom-call | tf_op jit(solution)/shard_map/pallas_call | solution.py:629

commit v5 on v4

--- a/solution.py
+++ b/solution.py
@@ -113,7 +113,7 @@
 def kernel(
     x_in, up_in, bank_in, queue_in, entry, slots, qkv_in, out_in, skip_in, gains,
     desc_ref, asc_ref,
-    xs, down, bank, queue, stage_qkv, act, wqv, wk, qt, kk, vt, qs, ks, vs, scores, ot, mt,
+    xs, down, bank, queue, stage_qkv, act, wqv, wk, qt, kk, vt, qs, ks, kt, vs, scores, ot, mt,
     wo, wsk, part_send, part_recv, x1, operand, give, asc_send, asc_recv, asc_out, own_up, early_peak, early_total,
     load, store, act_send, act_recv, wo_send, wo_recv, wsk_send, wsk_recv,
     pair_send, pair_recv, w_send, w_recv, head_send, head_recv,
@@ -151,10 +151,10 @@
 
     pad = HP - HEAD
     wo[:, HEAD:HP, :] = jnp.zeros((2 * RING, pad, D), BF)
-    for block in range(4):
+    for block in range(5):
         wqv[block * HP + HEAD : (block + 1) * HP, :] = jnp.zeros((pad, D), BF)
-    for block in range(2):
-        wk[block * 128 + HEAD : (block + 1) * 128, :] = jnp.zeros((128 - HEAD, D), BF)
+    wk[HEAD:128, :] = jnp.zeros((128 - HEAD, D), BF)
+    kt[:, HEAD:128, :] = jnp.zeros((2, 128 - HEAD, 1024), BF)
     qt[:, :, HEAD:128, :] = jnp.zeros((2, 2, 128 - HEAD, 1024), BF)
     mt[:, :, :, HEAD:HP, :] = jnp.zeros((2, 2, RING, pad, TOK), BF)
     ones = (lax.broadcasted_iota(jnp.int32, (pad, 2048), 0) == 0).astype(F32).astype(BF)
@@ -199,7 +199,7 @@
     w_copies = [
         to_partner(wqv.at[pl.ds(0, HEAD), :], wqv.at[pl.ds(2 * HP, HEAD), :], w_send.at[0], w_recv.at[0]),
         to_partner(wqv.at[pl.ds(HP, HEAD), :], wqv.at[pl.ds(3 * HP, HEAD), :], w_send.at[1], w_recv.at[1]),
-        to_partner(wk.at[pl.ds(0, HEAD), :], wk.at[pl.ds(128, HEAD), :], w_send.at[2], w_recv.at[2]),
+        to_partner(wk.at[pl.ds(0, HEAD), :], wqv.at[pl.ds(4 * HP, HEAD), :], w_send.at[2], w_recv.at[2]),
     ]
     give_copies = [
         to_partner(give.at[t], operand.at[t, pl.ds(TOK, TOK), :], give_ss.at[t], give_rs.at[t])
@@ -222,8 +222,8 @@
                 pair_send.at[t, g, 0], pair_recv.at[t, g, 0],
             ),
             to_partner(
-                ks.at[t, pl.ds(lo * TOK, n), :],
-                kk.at[t, pl.ds(1024 + lo * TOK, n), :],
+                ks.at[t, :, pl.ds(lo * TOK, n)],
+                kt.at[t, pl.ds(0, HEAD), pl.ds(lo * TOK, n)],
                 pair_send.at[t, g, 1], pair_recv.at[t, g, 1],
             ),
             to_partner(
@@ -246,10 +246,14 @@
         vt[t, 0:HEAD, lo * TOK : hi * TOK] = made[HP : HP + HEAD]
         qs[t, :, lo * TOK : hi * TOK] = pair_q
         vs[t, :, lo * TOK : hi * TOK] = made[3 * HP : 3 * HP + HEAD]
-        kk[t, lo * TOK : hi * TOK, :] = keys[:, 0:128]
-        ks[t, lo * TOK : hi * TOK, :] = keys[:, 128:256]
+        ks[t, :, lo * TOK : hi * TOK] = made[4 * HP : 4 * HP + HEAD]
+        kk[t, lo * TOK : hi * TOK, :] = keys
         for copy in pair_copies(t, g):
             copy.start()
+
+    def turn_keys(t, lo, hi):
+        for p in range(lo, hi):
+            kk[t, 1024 + p * TOK : 1024 + (p + 1) * TOK, :] = kt[t, :, p * TOK : (p + 1) * TOK].T
 
     def head_copy(t, half, p, mirror, delta):
         ring = 1 - y if t == 1 and half == 1 else y
@@ -403,6 +407,7 @@
     for g in range(5):
         for copy in pair_copies(0, g):
             copy.wait_recv()
+    turn_keys(0, 0, 8)
     swap_copy(0).start()
 
     def out_step(j):
@@ -499,6 +504,7 @@
     for g in range(4):
         for copy in pair_copies(1, g):
             copy.wait_recv()
+    turn_keys(1, 0, 7)
 
     def early(i, carry):
         attend_early(2 - i)
@@ -508,6 +514,7 @@
     lax.fori_loop(0, 3, early, 0)
     for copy in pair_copies(1, 4):
         copy.wait_recv()
+    turn_keys(1, 7, 8)
     attend(1, 1, 0, 1, {})
     attend(1, 1, 1, 4, {}, attend_late)
     attend(1, 0, 0, 4, {})
@@ -580,13 +587,14 @@
         V((8, TOK, D), BF),
         V((3, HEAD, D), BF),
         V((2, RING, TOK, D), BF),
-        V((4 * HP, D), BF),
-        V((256, D), BF),
+        V((5 * HP, D), BF),
+        V((TOK, D), BF),
         V((2, 2, 128, 1024), BF),
         V((2, 2048, 128), BF),
         V((2, HP, 2048), BF),
         V((2, HEAD, 1024), BF),
-        V((2, 1024, 128), BF),
+        V((2, HEAD, 1024), BF),
+        V((2, 128, 1024), BF),
         V((2, HEAD, 1024), BF),
         V((8, 256, 256), F32),
         V((2, 2, RING, HEAD, TOK), BF),

time: 165 us -> 165 us (level)
  no operation moved by 1% of the time
where the time goes in v5:
time: 165 us; the launch traced here: 162 us
  Pallas kernels  162 us (98%)
    pallas_call x1, Pallas kernels, on_device(): pl.pallas_call(kernel, out_shape=(jax.ShapeDtypeStruct((2, TOK, D), BF),...  159 us

profile of v5, /device:TPU:2, one launch (start us, length us, event | category | flops | bytes accessed | tf_op | source)
XLA Modules:
  0.0 162.4 jit_solution(1216066668529628104)
XLA Ops:
  0.6 159.3 %shard_map.113 = (bf16[2,128,1408]{2,1,0:T(8,128)(2,1)}, bf16[2,128,1408]{2,1,0:T(8,128)(2,1)}) custom-call(bf16[128,1408]{1,0:T(8,128)(2,1)} %bitcast.17, bf16[128,1408]{1,0:T(8,128)(2,1)} %bitcast.18, bf16[3,128,1408]{2,1,0:T(8,128)(2,1)} %bitcast.14, bf16[8,128,1408]{2,1,0:T(8,128)(2,1)} %queue_in.1, s32[8]{0:T(128)} %entry.1, s32[1,2]{1,0:T(1,128)} %bitcast.21, ...), custom_call_target="tpu_custom_call" | custom-call | tf_op jit(solution)/shard_map/pallas_call | solution.py:621
  160.0 2.2 %shard_map.114 = (bf16[2,128,1408]{2,1,0:T(8,128)(2,1)}, bf16[2,128,1408]{2,1,0:T(8,128)(2,1)}) custom-call(bf16[2,128,1408]{2,1,0:T(8,128)(2,1)} %get-tuple-element.6.desc_in, bf16[2,128,1408]{2,1,0:T(8,128)(2,1)} %get-tuple-element.7.asc_in), custom_call_target="tpu_custom_call" | custom-call | tf_op jit(solution)/shard_map/pallas_call | solution.py:637
